TPU v7x, 256 devices: a whole 4x4x8 slice. The times are simulated.
256 devices in a mesh: blk: 64 (over y, x_hi, z), az: 4 (over x_lo, core).
Axes of the slice: x: 4 (x_hi: 2, x_lo: 2; x = x_hi * 2 + x_lo), y: 4, z: 8, core: 2. Of those that a mesh axis runs over, the one named last changes fastest.
Arguments:
- lower_part: float32 [64, 512, 512], P('blk', None, 'az'), may hold values from -0.02 to 0.02
- diag_part: float32 [64, 512, 512], P('blk', None, 'az'), may hold values from -0.02 to 0.02
- upper_part: float32 [64, 512, 512], P('blk', None, 'az'), may hold values from -0.02 to 0.02
- right_side: float32 [64, 512, 512], P('blk', None, 'az'), may hold values from -6 to 6
- extra: float32 [32768, 512], P('blk', 'az'), may hold values from -6 to 6
- owners: int32 [32768, 1], P('blk'), may hold values from 0 to 63; in each aligned block of 512 rows (0 to 511, 512 to 1023, ...) at most 16 rows name the same one
- rows_in: int32 [32768], P('blk'), may hold values from 0 to 511
- counts: int32 [64], P('blk'), may hold values from 384 to 512, as said below
Outputs:
- solution: float32 [64, 512, 512], P('blk', None, 'az')
Inputs may be any that keep to these rules, and one draw needn't show every extreme that they name: `owners`: within the 512 entries of one subdomain no block row is named more than 16 times; some subdomain names some block row exactly 16 times. `counts`: A subdomain's entries at positions below its count are live, the others are ignored; some subdomain has all 512 entries live.
All inputs are finite; a program needn't handle non-finite values.
Results may differ from a plain program's by a relative error of at most 0.00013.
Values sent between devices are 32-bit elements; how exact they have to be, the bound alone decides.
A program may use at most 64 MiB of HBM per device.

v0:
```python
import functools

import jax
import jax.numpy as jnp
from jax import lax
from jax.experimental import pallas as pl
from jax.experimental.pallas import tpu as pltpu
from jax.sharding import PartitionSpec as P

coupling = 0.42
MESH = pl.DeviceIdType.MESH
LEVELS = 4
F32, BF16 = jnp.float32, jnp.bfloat16


def product(left, right):
    return jnp.dot(left, right, precision=lax.Precision.HIGHEST, preferred_element_type=jnp.float32)


def deliver(extra, owners, rows_in, counts, block_order):
    cycle_size = lax.axis_size("blk")
    entries = owners.shape[0]
    slot_count = 2 * entries // cycle_size
    owner_ids = owners[:, 0]
    position = lax.iota(jnp.int32, entries)
    live_mask = position < counts[0]
    earlier_same = (
        (owner_ids[:, None] == owner_ids[None, :])
        & live_mask[None, :]
        & (position[None, :] < position[:, None])
    )
    slot_rank = jnp.sum(earlier_same.astype(jnp.int32), axis=1)
    target = jnp.where(live_mask, owner_ids * slot_count + slot_rank, cycle_size * slot_count)
    local_width = extra.shape[1]
    send_values = (
        jnp.zeros((cycle_size * slot_count, local_width), jnp.float32)
        .at[target]
        .set(extra, mode="drop")
    )
    row_marks = (
        jnp.full((cycle_size * slot_count,), -1.0, jnp.float32)
        .at[target]
        .set(rows_in.astype(jnp.float32), mode="drop")
    )
    got_values, got_marks = (
        lax.all_to_all(
            send_values.reshape(cycle_size, slot_count, local_width),
            "blk",
            split_axis=0,
            concat_axis=0,
            tiled=True,
        ),
        lax.all_to_all(
            row_marks.reshape(cycle_size, slot_count),
            "blk",
            split_axis=0,
            concat_axis=0,
            tiled=True,
        ),
    )
    got_values = got_values.reshape(cycle_size * slot_count, local_width)
    got_marks = got_marks.reshape(cycle_size * slot_count)
    row_grid = lax.broadcasted_iota(jnp.int32, (block_order, cycle_size * slot_count), 0).astype(
        jnp.float32
    )
    onehot = (row_grid == got_marks[None, :]).astype(jnp.float32)
    return product(onehot, got_values)


def halves(x):
    hi = x.astype(BF16)
    return hi, (x - hi.astype(F32)).astype(BF16)


def mm(a, b):
    return jnp.dot(a, b, preferred_element_type=F32)


def kernel(
    l_ref, d_ref, u_ref, b_ref, o_ref,
    gath, blocks, sent, got, dh, dl, luh, lul, vh, vl, xh, xl, w_ref, rh, bcur,
    gs, gr, es, er,
):
    n = d_ref.shape[0]
    c = d_ref.shape[1]
    tile = n // 2
    tiles = [pl.ds(t * tile, tile) for t in range(2)]
    blk = lax.axis_index("blk")
    az = lax.axis_index("az")
    cycle = lax.axis_size("blk")
    mate = (az // 2) * 2 + 1 - az % 2
    across = (az + 2) % 4
    diag = (mate + 2) % 4

    def lower(s):
        return (blk - s + cycle) % cycle

    def upper(s):
        return (blk + s) % cycle

    peers = [(blk, mate), (blk, across)]
    for k in range(LEVELS):
        peers += [(lower(2**k), az), (upper(2**k), az)]
    barrier = pltpu.get_barrier_semaphore()
    for peer in peers:
        pl.semaphore_signal(barrier, inc=1, device_id=peer, device_id_type=MESH)
    pl.semaphore_wait(barrier, len(peers))

    started = []

    def gather_copy(k, m, which, slot, device):
        return pltpu.make_async_remote_copy(
            src_ref=gath.at[k, m, slot], dst_ref=gath.at[k, m, slot],
            send_sem=gs.at[k, m, which], recv_sem=gr.at[k, m, which],
            device_id=device, device_id_type=MESH,
        )

    def gather_start(k, m):
        one = gather_copy(k, m, 0, az, (blk, mate))
        two = gather_copy(k, m, 1, az, (blk, across))
        two.start()
        one.start()
        started.extend([one, two])

    def gather_finish(k, m, into_h, into_l, base):
        def put(slot):
            col = pl.ds(pl.multiple_of(base + slot * c, c), c)
            hi, lo = halves(gath[k, m, slot])
            into_h[:, col] = hi
            into_l[:, col] = lo

        put(az)
        gather_copy(k, m, 0, mate, (blk, mate)).wait_recv()
        put(mate)
        gather_copy(k, m, 1, across, (blk, across)).wait_recv()
        three = gather_copy(k, m, 2, across, (blk, mate))
        three.start()
        started.append(three)
        put(across)
        gather_copy(k, m, 2, diag, (blk, mate)).wait_recv()
        put(diag)

    def send(k, which, slot, target):
        copy = pltpu.make_async_remote_copy(
            src_ref=sent.at[k, slot], dst_ref=got.at[k, which],
            send_sem=es.at[k, which], recv_sem=er.at[k, which],
            device_id=(target, az), device_id_type=MESH,
        )
        copy.start()
        started.append(copy)

    def arrived(k, which):
        pltpu.make_async_remote_copy(
            src_ref=sent.at[k, 0], dst_ref=got.at[k, which],
            send_sem=es.at[k, which], recv_sem=er.at[k, which],
            device_id=(blk, az), device_id_type=MESH,
        ).wait_recv()

    def apply_wide(k):
        for part, m in ((0, 1), (1, 2)):
            col = slice(part * c, (part + 1) * c)
            hi, lo = halves(gath[k, m, az])
            vh[:, col] = hi
            vl[:, col] = lo

        def times(rows, hi, lo):
            return mm(dh[rows, :], hi) + mm(dh[rows, :], lo) + mm(dl[rows, :], hi)

        def base(rows):
            return jnp.concatenate([gath[k, 1, az, rows, :], gath[k, 2, az, rows, :]], axis=1)

        for rows in tiles:
            x = 2.0 * base(rows) - times(rows, vh[...], vl[...])
            xh[rows, :], xl[rows, :] = halves(x)
        for rows in tiles:
            w = 2.0 * base(rows) - times(rows, xh[...], xl[...])
            w_ref[rows, :] = w
            vh[rows, :], vl[rows, :] = halves(w)
        for rows in tiles:
            out = 2.0 * w_ref[rows, :] - times(rows, vh[...], vl[...])
            sent[k, 0, rows, :] = out[:, :c]
            sent[k, 1, rows, :] = out[:, c:]

    def narrow(rows, ah, al, pair):
        both = mm(ah[rows, :], pair)
        return both[:, :c] + both[:, c:] + mm(al[rows, :], pair[:, :c])

    def put_pair(ref, rows, x):
        ref[rows, :c], ref[rows, c:] = halves(x)

    def apply_narrow(v_ref, write):
        put_pair(vh, slice(None), v_ref[...])
        for rows in tiles:
            put_pair(xh, rows, 2.0 * v_ref[rows, :] - narrow(rows, dh, dl, vh[...]))
        for rows in tiles:
            w = 2.0 * v_ref[rows, :] - narrow(rows, dh, dl, xh[...])
            w_ref[rows, :c] = w
            put_pair(vh, rows, w)
        for rows in tiles:
            write(rows, 2.0 * w_ref[rows, :c] - narrow(rows, dh, dl, vh[...]))

    def combined(k, first, second, old, write):
        p = k % 2
        put_pair(rh, slice(0, n), got[k, first])
        put_pair(rh, slice(n, 2 * n), got[k, second])
        for rows in tiles:
            pair = rh[...]
            both = mm(luh[p, rows, :], pair)
            value = both[:, :c] + both[:, c:] + mm(lul[p, rows, :], pair[:, :c])
            write(rows, old[rows, :] - value)

    def single(k, which, side, write):
        p = k % 2
        put_pair(rh, slice(0, n), got[k, which])
        col = slice(side * n, (side + 1) * n)
        for rows in tiles:
            pair = rh[0:n, :]
            both = mm(luh[p, rows, col], pair)
            value = both[:, :c] + both[:, c:] + mm(lul[p, rows, col], pair[:, :c])
            write(rows, -value)

    def store(ref):
        def write(rows, value):
            ref[rows, :] = value

        return write

    eye = (
        lax.broadcasted_iota(jnp.int32, (n, c), 0) == lax.broadcasted_iota(jnp.int32, (n, c), 1) + az * c
    ).astype(F32)
    gath[0, 0, az] = d_ref[...] + eye
    gather_start(0, 0)
    gath[0, 1, az] = l_ref[...] - coupling * eye
    gather_start(0, 1)
    gath[0, 2, az] = u_ref[...] - coupling * eye
    gather_start(0, 2)

    QM, PP, PM, QP, YM, YP = range(6)
    for k in range(LEVELS):
        s = 2**k
        last = k == LEVELS - 1
        gather_finish(k, 0, dh, dl, 0)
        apply_wide(k)
        send(k, QM, 1, upper(s))
        send(k, PP, 0, lower(s))
        if not last:
            send(k, PM, 0, upper(s))
            send(k, QP, 1, lower(s))
        if k == 0:
            bcur[0] = b_ref[...]
        else:
            arrived(k - 1, YM)
            arrived(k - 1, YP)
            combined(k - 1, YM, YP, bcur.at[(k - 1) % 2], store(bcur.at[k % 2]))
        apply_narrow(bcur.at[k % 2], store(sent.at[k, 2]))
        send(k, YM, 2, upper(s))
        send(k, YP, 2, lower(s))
        gather_finish(k, 1, luh.at[k % 2], lul.at[k % 2], 0)
        gather_finish(k, 2, luh.at[k % 2], lul.at[k % 2], n)
        arrived(k, QM)
        arrived(k, PP)
        combined(k, QM, PP, gath.at[k, 0, az], store(gath.at[k + 1, 0, az]))
        gather_start(k + 1, 0)
        if not last:
            arrived(k, PM)
            single(k, PM, 0, store(gath.at[k + 1, 1, az]))
            gather_start(k + 1, 1)
            arrived(k, QP)
            single(k, QP, 1, store(gath.at[k + 1, 2, az]))
            gather_start(k + 1, 2)
    gather_finish(LEVELS, 0, dh, dl, 0)
    arrived(LEVELS - 1, YM)
    arrived(LEVELS - 1, YP)
    combined(LEVELS - 1, YM, YP, bcur.at[(LEVELS - 1) % 2], store(bcur.at[LEVELS % 2]))
    apply_narrow(bcur.at[LEVELS % 2], store(o_ref))
    for copy in started:
        copy.wait_send()


def on_device(lower_part, diag_part, upper_part, right_side, extra, owners, rows_in, counts):
    n, c = diag_part.shape[1:]
    right_block = right_side[0] + deliver(extra, owners, rows_in, counts, n)
    vmem = pl.BlockSpec(memory_space=pltpu.VMEM)
    out = pl.pallas_call(
        kernel,
        name="levels",
        out_shape=jax.ShapeDtypeStruct((n, c), F32),
        in_specs=[vmem] * 4,
        out_specs=vmem,
        scratch_shapes=[
            pltpu.VMEM((LEVELS + 1, 3, 4, n, c), F32),
            pltpu.VMEM((8, 128), F32),
            pltpu.VMEM((LEVELS, 3, n, c), F32),
            pltpu.VMEM((LEVELS, 6, n, c), F32),
            pltpu.VMEM((n, n), BF16),
            pltpu.VMEM((n, n), BF16),
            pltpu.VMEM((2, n, 2 * n), BF16),
            pltpu.VMEM((2, n, 2 * n), BF16),
            pltpu.VMEM((n, 2 * c), BF16),
            pltpu.VMEM((n, 2 * c), BF16),
            pltpu.VMEM((n, 2 * c), BF16),
            pltpu.VMEM((n, 2 * c), BF16),
            pltpu.VMEM((n, 2 * c), F32),
            pltpu.VMEM((2 * n, 2 * c), BF16),
            pltpu.VMEM((2, n, c), F32),
            pltpu.SemaphoreType.DMA((LEVELS + 1, 3, 3)),
            pltpu.SemaphoreType.DMA((LEVELS + 1, 3, 3)),
            pltpu.SemaphoreType.DMA((LEVELS, 6)),
            pltpu.SemaphoreType.DMA((LEVELS, 6)),
        ],
        compiler_params=pltpu.CompilerParams(
            collective_id=0, has_side_effects=True, vmem_limit_bytes=56 * 2**20
        ),
    )(lower_part[0], diag_part[0], upper_part[0], right_block)
    return out[None]


def solution(mesh):
    placed = (
        P("blk", None, "az"),
        P("blk", None, "az"),
        P("blk", None, "az"),
        P("blk", None, "az"),
        P("blk", "az"),
        P("blk", None),
        P("blk"),
        P("blk"),
    )
    return jax.shard_map(
        on_device, mesh=mesh, in_specs=placed, out_specs=P("blk", None, "az"), check_vma=False
    )
```

profile of v0, /device:TPU:173, one launch (start us, length us, event | category | flops | bytes accessed | tf_op | source)
XLA Modules:
  0.0 258.4 jit_solution(18346715659199423860)
XLA Ops:
  0.7 0.7 convert_element_type.13
  1.4 1.0 convert_reduce_fusion
  2.4 0.7 compare_select_fusion
  3.1 2.4 scatter_custom_fusion
  5.5 0.7 all_to_all.9
  6.2 11.7 %all-to-all-start = ((f32[64,1,16]{2,1,0:T(1,128)}), f32[64,1,16]{2,1,0:T(1,128)S(1)}, u32[]{:S(2)}, u32[]{:S(2)}) async-start(f32[64,1,16]{2,1,0:T(1,128)} %bitcast.8), calls=%async_computation | async-start | bytes 65536 | tf_op jit(solution)/shard_map/all_to_all | solution.py:53
  18.0 2.9 %scatter_custom_fusion.1 = f32[1024,128]{1,0:T(8,128)} fusion(s32[512]{0:T(512)S(1)} %bitcast.24, f32[512,128]{1,0:T(8,128)} %param.12, f32[]{:T(128)} %constant.2.clone.1), kind=kCustom, calls=%fused_computation.10 | custom fusion | bytes 524800 | tf_op jit(solution)/shard_map/scatter | solution.py:38
  20.8 1.0 all-to-all-done
  21.8 0.0 copy-start
  21.8 11.8 %all-to-all-start.1 = ((f32[64,16,128]{2,1,0:T(8,128)}), f32[64,16,128]{2,1,0:T(8,128)S(1)}, u32[]{:S(2)}, u32[]{:S(2)}) async-start(f32[64,16,128]{2,1,0:T(8,128)} %bitcast.9), calls=%async_computation.1 | async-start | bytes 1048576 | tf_op jit(solution)/shard_map/all_to_all | solution.py:46
  33.6 0.5 broadcast.25
  34.2 0.7 reduce.3
  34.9 0.1 eq.29
  35.0 10.6 %all-to-all-done.1 = f32[64,16,128]{2,1,0:T(8,128)S(1)} async-done(((f32[64,16,128]{2,1,0:T(8,128)}), f32[64,16,128]{2,1,0:T(8,128)S(1)}, u32[]{:S(2)}, u32[]{:S(2)}) %all-to-all-start.1) | async-done | bytes 524320 | tf_op jit(solution)/shard_map/all_to_all | solution.py:46
  45.6 0.0 copy-done
  45.6 1.8 fusion.2.b_ref
  47.4 209.3 %levels.1 = f32[512,128]{1,0:T(8,128)} custom-call(f32[512,128]{1,0:T(8,128)} %bitcast.18, f32[512,128]{1,0:T(8,128)} %bitcast.19, f32[512,128]{1,0:T(8,128)} %bitcast.20, f32[512,128]{1,0:T(8,128)} %fusion.2.b_ref), custom_call_target="tpu_custom_call" | custom-call | tf_op jit(solution)/shard_map/levels/pallas_call | solution.py:284
  256.7 1.7 copy.13
  (2 shorter events, 0.0 us)
Async XLA Ops:
  6.2 15.6 %all-to-all-start = ((f32[64,1,16]{2,1,0:T(1,128)}), f32[64,1,16]{2,1,0:T(1,128)S(1)}, u32[]{:S(2)}, u32[]{:S(2)}) async-start(f32[64,1,16]{2,1,0:T(1,128)} %bitcast.8), calls=%async_computation | async-start | bytes 65536 | tf_op jit(solution)/shard_map/all_to_all | solution.py:53
  21.8 23.8 %copy-start = (f32[1,512,128]{2,1,0:T(8,128)S(1)}, f32[1,512,128]{2,1,0:T(8,128)}, u32[]{:S(2)}) copy-start(f32[1,512,128]{2,1,0:T(8,128)} %param.11) | copy-start | bytes 786436
  21.8 23.8 %all-to-all-start.1 = ((f32[64,16,128]{2,1,0:T(8,128)}), f32[64,16,128]{2,1,0:T(8,128)S(1)}, u32[]{:S(2)}, u32[]{:S(2)}) async-start(f32[64,16,128]{2,1,0:T(8,128)} %bitcast.9), calls=%async_computation.1 | async-start | bytes 1048576 | tf_op jit(solution)/shard_map/all_to_all | solution.py:46
where the time goes:
time: 259 us; the launch traced here: 258 us
  Pallas kernels  209 us (81%)
  starting transfers between devices  23.5 us (9%)
  waiting for transfers between devices  11.7 us (5%)
  local copies, waits for them, and re-layouts  8.27 us (3%)
  other arithmetic  3.14 us (1%)
    pallas_call x1, Pallas kernels, on_device(): pl.pallas_call(kernel, name='levels', out_shape=jax.ShapeDtypeStruct((n,...  209 us
    all_to_all x1, starting transfers between devices, deliver(): lax.all_to_all(send_values.reshape(cycle_size, slot_count, local_width),...  11.8 us
    all_to_all x1, starting transfers between devices, deliver(): lax.all_to_all(row_marks.reshape(cycle_size, slot_count), 'blk', split_ax...  11.7 us
    all_to_all x1, waiting for transfers between devices, deliver(): lax.all_to_all(send_values.reshape(cycle_size, slot_count, local_width),...  10.6 us
  transfers between devices with their start and end apart: 2, of which 2 were waited for; matrix products, arithmetic and copies ran while one was open for 2% of the time, Pallas kernels for 0%

commit v1 on v0

v1 whole, which is shorter than its diff:
```python
import functools

import jax
import jax.numpy as jnp
from jax import lax
from jax.experimental import pallas as pl
from jax.experimental.pallas import tpu as pltpu
from jax.sharding import PartitionSpec as P

coupling = 0.42
MESH = pl.DeviceIdType.MESH
LEVELS = 4
RING = 8
F32, BF16 = jnp.float32, jnp.bfloat16


def halves(x):
    hi = x.astype(BF16)
    return hi, (x - hi.astype(F32)).astype(BF16)


def mm(a, b):
    return jnp.dot(a, b, preferred_element_type=F32)


def kernel(
    l_ref, d_ref, u_ref, b_ref, x_ref, own_ref, row_ref, cnt_ref, o_ref,
    gath, sent, got, dh, dl, luh, lul, vh, vl, xh, xl, w_ref, rh, bcur,
    out_v, out_m, in_v, in_m, swap, gs, gr, es, er, ps, ws, wr,
):
    n = d_ref.shape[0]
    c = d_ref.shape[1]
    tile = n // 2
    tiles = [pl.ds(t * tile, tile) for t in range(2)]
    blk = lax.axis_index("blk")
    az = lax.axis_index("az")
    cycle = lax.axis_size("blk")
    mate = (az // 2) * 2 + 1 - az % 2
    across = (az + 2) % 4
    odd = (blk // RING) % 2
    col = (az + 2 * odd) % 4

    def lower(s):
        return (blk - s + cycle) % cycle

    def upper(s):
        return (blk + s) % cycle

    def at(row):
        return (row, (col + 2 * ((row // RING) % 2)) % 4)

    entries = x_ref.shape[0]
    slots = out_v.shape[0] // cycle
    barrier = pltpu.get_barrier_semaphore()
    pl.semaphore_signal(barrier, inc=1, device_id=(blk, mate), device_id_type=MESH)
    pl.semaphore_signal(barrier, inc=1, device_id=(blk, across), device_id_type=MESH)

    @pl.loop(1, cycle)
    def _(step):
        to = upper(step)
        pl.semaphore_signal(barrier, inc=1, device_id=(to, az), device_id_type=MESH)
        pl.semaphore_signal(barrier, inc=1, device_id=(to, (az + 2) % 4), device_id_type=MESH)

    started = []

    def gather_copy(k, m, which, slot, device):
        return pltpu.make_async_remote_copy(
            src_ref=gath.at[k, m, slot], dst_ref=gath.at[k, m, slot],
            send_sem=gs.at[k, m, which], recv_sem=gr.at[k, m, which],
            device_id=device, device_id_type=MESH,
        )

    def gather_start(k, m):
        mine = az if k == 0 else col
        one = gather_copy(k, m, 0, mine, (blk, mate))
        two = gather_copy(k, m, 1, mine, (blk, across))
        two.start()
        one.start()
        started.extend([one, two])

    def gather_finish(k, m, into_h, into_l, base):
        mine = az if k == 0 else col
        beside = (mine // 2) * 2 + 1 - mine % 2

        def put(slot):
            where = pl.ds(pl.multiple_of(base + slot * c, c), c)
            hi, lo = halves(gath[k, m, slot])
            into_h[:, where] = hi
            into_l[:, where] = lo

        put(mine)
        gather_copy(k, m, 0, beside, (blk, mate)).wait_recv()
        put(beside)
        gather_copy(k, m, 1, (mine + 2) % 4, (blk, across)).wait_recv()
        three = gather_copy(k, m, 2, (mine + 2) % 4, (blk, mate))
        three.start()
        started.append(three)
        put((mine + 2) % 4)
        gather_copy(k, m, 2, (beside + 2) % 4, (blk, mate)).wait_recv()
        put((beside + 2) % 4)

    def swap_copy(which, src):
        return pltpu.make_async_remote_copy(
            src_ref=src, dst_ref=swap.at[which, 1], send_sem=ws.at[which], recv_sem=wr.at[which],
            device_id=(blk, across), device_id_type=MESH,
        )

    def swap_start(which, src):
        swap[which, 0] = src[...]

        @pl.when(odd == 1)
        def _():
            swap_copy(which, swap.at[which, 0]).start()

    def swap_finish(which):
        @pl.when(odd == 1)
        def _():
            swap_copy(which, swap.at[which, 0]).wait()

    def send(k, which, slot, target):
        copy = pltpu.make_async_remote_copy(
            src_ref=sent.at[k, slot], dst_ref=got.at[k, which],
            send_sem=es.at[k, slot, which // 3], recv_sem=er.at[k, which],
            device_id=target, device_id_type=MESH,
        )
        copy.start()
        started.append(copy)
        return copy

    def arrived(k, which):
        pltpu.make_async_remote_copy(
            src_ref=sent.at[k, 0], dst_ref=got.at[k, which],
            send_sem=er.at[k, which], recv_sem=er.at[k, which],
            device_id=(blk, az), device_id_type=MESH,
        ).wait_recv()

    half = (blk % RING) // (RING // 2)
    near = (blk // RING) * RING + (blk + RING // 2) % RING
    far = (blk + RING * (1 - 2 * half) + cycle) % cycle

    def send_shared(k, slot):
        copy = pltpu.make_async_remote_copy(
            src_ref=sent.at[k, slot], dst_ref=got.at[k, half * 3 + slot],
            send_sem=es.at[k, slot, 0], recv_sem=er.at[k, half * 3 + slot],
            device_id=at(near), device_id_type=MESH,
        )
        copy.start()
        started.append(copy)

    def pass_on(k, slot):
        direct = (1 - half) * 3 + slot
        arrived(k, direct)
        copy = pltpu.make_async_remote_copy(
            src_ref=got.at[k, direct], dst_ref=got.at[k, half * 3 + slot],
            send_sem=es.at[k, slot, 1], recv_sem=er.at[k, half * 3 + slot],
            device_id=at(far), device_id_type=MESH,
        )
        copy.start()
        started.append(copy)

    def arrived_shared(k, slot):
        arrived(k, half * 3 + slot)

    def apply_wide(k):
        for part, m in ((0, 1), (1, 2)):
            hi, lo = halves(gath[k, m, col])
            vh[:, part * c : (part + 1) * c] = hi
            vl[:, part * c : (part + 1) * c] = lo

        def times(rows, hi, lo):
            return mm(dh[rows, :], hi) + mm(dh[rows, :], lo) + mm(dl[rows, :], hi)

        def base(rows):
            return jnp.concatenate([gath[k, 1, col, rows, :], gath[k, 2, col, rows, :]], axis=1)

        for rows in tiles:
            x = 2.0 * base(rows) - times(rows, vh[...], vl[...])
            xh[rows, :], xl[rows, :] = halves(x)
        for rows in tiles:
            w = 2.0 * base(rows) - times(rows, xh[...], xl[...])
            w_ref[rows, :] = w
            vh[rows, :], vl[rows, :] = halves(w)
        for rows in tiles:
            out = 2.0 * w_ref[rows, :] - times(rows, vh[...], vl[...])
            sent[k, 0, rows, :] = out[:, :c]
            sent[k, 1, rows, :] = out[:, c:]

    def narrow(rows, ah, al, pair):
        both = mm(ah[rows, :], pair)
        return both[:, :c] + both[:, c:] + mm(al[rows, :], pair[:, :c])

    def put_pair(ref, rows, x):
        ref[rows, :c], ref[rows, c:] = halves(x)

    def apply_narrow(v_ref, write):
        put_pair(vh, slice(None), v_ref[...])
        for rows in tiles:
            put_pair(xh, rows, 2.0 * v_ref[rows, :] - narrow(rows, dh, dl, vh[...]))
        for rows in tiles:
            w = 2.0 * v_ref[rows, :] - narrow(rows, dh, dl, xh[...])
            w_ref[rows, :c] = w
            put_pair(vh, rows, w)
        for rows in tiles:
            write(rows, 2.0 * w_ref[rows, :c] - narrow(rows, dh, dl, vh[...]))

    def combined(k, first, second, old, write):
        p = k % 2
        put_pair(rh, slice(0, n), got[k, first])
        put_pair(rh, slice(n, 2 * n), got[k, second])
        for rows in tiles:
            pair = rh[...]
            both = mm(luh[p, rows, :], pair)
            value = both[:, :c] + both[:, c:] + mm(lul[p, rows, :], pair[:, :c])
            write(rows, old[rows, :] - value)

    def single(k, which, side, write):
        p = k % 2
        put_pair(rh, slice(0, n), got[k, which])
        cols = slice(side * n, (side + 1) * n)
        for rows in tiles:
            pair = rh[0:n, :]
            both = mm(luh[p, rows, cols], pair)
            value = both[:, :c] + both[:, c:] + mm(lul[p, rows, cols], pair[:, :c])
            write(rows, -value)

    def store(ref):
        def write(rows, value):
            ref[rows, :] = value

        return write

    def pack():
        live = lax.broadcasted_iota(jnp.int32, (1, entries), 1) < cnt_ref[...]
        owner = jnp.where(live, own_ref[...], -1)
        named = jnp.where(lax.broadcasted_iota(jnp.int32, (cycle, entries), 0) == owner, 1.0, 0.0)
        earlier = jnp.where(
            lax.broadcasted_iota(jnp.int32, (entries, entries), 0)
            < lax.broadcasted_iota(jnp.int32, (entries, entries), 1), 1.0, 0.0
        ).astype(BF16)
        before = mm(named.astype(BF16), earlier)
        rank = jnp.sum(named * before, axis=0, keepdims=True).astype(jnp.int32)
        target = jnp.where(live, owner * slots + rank, -1)
        row = row_ref[...]
        place = lax.broadcasted_iota(jnp.int32, (128, entries), 0)
        marks = jnp.where(place == rank, row // slots, jnp.where(place == rank + slots, row % slots, 0))
        out_m[...] = lax.dot_general(
            named.astype(BF16), marks.astype(F32).astype(BF16), (((1,), (1,)), ((), ())),
            preferred_element_type=F32,
        )[:, None, :]
        put_pair(vh, slice(None), x_ref[...])
        part = 256
        for t in range(out_v.shape[0] // part):
            pick = jnp.where(
                lax.broadcasted_iota(jnp.int32, (part, entries), 0) + t * part == target, 1.0, 0.0
            ).astype(BF16)
            both = mm(pick, vh[...])
            out_v[t * part : (t + 1) * part, :] = both[:, :c] + both[:, c:]

    def block_of(ref, index):
        return ref.at[pl.ds(pl.multiple_of(index * slots, slots), slots), :]

    def deliver():
        pltpu.make_async_copy(out_m.at[blk], in_m.at[blk], ps.at[3]).start()

        @pl.when(odd == 0)
        def _():
            pltpu.make_async_copy(block_of(out_v, blk), block_of(in_v, blk), ps.at[1]).start()

        @pl.when(odd == 1)
        def _():
            pltpu.make_async_remote_copy(
                src_ref=block_of(out_v, blk), dst_ref=block_of(in_v, blk), send_sem=ps.at[4], recv_sem=ps.at[1],
                device_id=(blk, across), device_id_type=MESH,
            ).start()

        @pl.loop(1, cycle)
        def _(step):
            to = upper(step)
            pltpu.make_async_remote_copy(
                src_ref=out_m.at[to], dst_ref=in_m.at[blk], send_sem=ps.at[2], recv_sem=ps.at[3],
                device_id=(to, (az + 2 * ((to // RING) % 2)) % 4), device_id_type=MESH,
            ).start()
            pltpu.make_async_remote_copy(
                src_ref=block_of(out_v, to), dst_ref=block_of(in_v, blk), send_sem=ps.at[0], recv_sem=ps.at[1],
                device_id=(to, (az + 2 * ((to // RING) % 2)) % 4), device_id_type=MESH,
            ).start()

    def unpack():
        pltpu.make_async_copy(in_m, in_m, ps.at[3]).wait()
        pltpu.make_async_copy(in_v, in_v, ps.at[1]).wait()
        total = in_v.shape[0]
        lane = lax.broadcasted_iota(jnp.int32, (128, total), 0)
        slot = lax.broadcasted_iota(jnp.int32, (128, total), 1) % slots
        spread = jnp.where(slot == lane, float(slots), jnp.where(slot + slots == lane, 1.0, 0.0))
        wide = mm(in_m[:, 0, :].astype(BF16), spread.astype(BF16))
        mine = lax.broadcasted_iota(jnp.int32, (cycle, total), 1) // slots == lax.broadcasted_iota(
            jnp.int32, (cycle, total), 0
        )
        mark = jnp.sum(jnp.where(mine, wide, 0.0), axis=0, keepdims=True).astype(jnp.int32)
        put_pair(rh, slice(None), in_v[...])
        for rows in tiles:
            pick = jnp.where(
                lax.broadcasted_iota(jnp.int32, (tile, total), 0) + rows.start == mark, 1.0, 0.0
            ).astype(BF16)
            both = mm(pick, rh[...])
            bcur[0, rows, :] = swap[0, odd, rows, :] + both[:, :c] + both[:, c:]

    eye = (
        lax.broadcasted_iota(jnp.int32, (n, c), 0) == lax.broadcasted_iota(jnp.int32, (n, c), 1) + az * c
    ).astype(F32)
    gath[0, 0, az] = d_ref[...] + eye
    gath[0, 1, az] = l_ref[...] - coupling * eye
    gath[0, 2, az] = u_ref[...] - coupling * eye
    pack()
    pl.semaphore_wait(barrier, 2 * cycle)
    for m in range(3):
        gather_start(0, m)

    PM, QM, YM, PP, QP, YP = range(6)
    rhs = []

    def right_side(k):
        s = 2**k
        last = k == LEVELS - 1
        shared = s == RING // 2
        if k == 0:
            swap_finish(0)
            unpack()
        else:
            if s == RING:
                arrived_shared(k - 1, 2)
            else:
                arrived(k - 1, YM)
                arrived(k - 1, YP)
            combined(k - 1, YM, YP, bcur.at[(k - 1) % 2], store(bcur.at[k % 2]))
        if last:
            swap_start(1, bcur.at[k % 2])
        apply_narrow(bcur.at[k % 2], store(sent.at[k, 2]))
        if shared:
            send_shared(k, 2)
        else:
            rhs[:] = [
                send(k, YM, 2, (upper(s), col) if last else at(upper(s))),
                send(k, YP, 2, (lower(s), col) if last else at(lower(s))),
            ]

    for k in range(LEVELS):
        s = 2**k
        last = k == LEVELS - 1
        shared = s == RING // 2
        gather_finish(k, 0, dh, dl, 0)
        if s == RING:
            pass_on(k - 1, 2)
        if k == 0:
            gather_finish(k, 1, luh.at[k % 2], lul.at[k % 2], 0)
            apply_narrow(gath.at[k, 1, col], store(sent.at[k, 0]))
            send(k, PP, 0, at(lower(s)))
            send(k, PM, 0, at(upper(s)))
            swap_start(0, b_ref)
            deliver()
            gather_finish(k, 2, luh.at[k % 2], lul.at[k % 2], n)
            apply_narrow(gath.at[k, 2, col], store(sent.at[k, 1]))
            send(k, QM, 1, at(upper(s)))
            send(k, QP, 1, at(lower(s)))
        else:
            apply_wide(k)
        if k == 0:
            pass
        elif shared:
            for copy in rhs:
                copy.wait_send()
            started[:] = [copy for copy in started if not any(copy is other for other in rhs)]
            send_shared(k, half)
            send_shared(k, 1 - half)
        else:
            send(k, QM, 1, at(upper(s)))
            send(k, PP, 0, at(lower(s)))
            if not last:
                send(k, PM, 0, at(upper(s)))
                send(k, QP, 1, at(lower(s)))
        if k > 0:
            right_side(k)
        if k > 0:
            gather_finish(k, 1, luh.at[k % 2], lul.at[k % 2], 0)
            gather_finish(k, 2, luh.at[k % 2], lul.at[k % 2], n)
        if shared:
            pass_on(k, 1 - half)
            pass_on(k, half)
            arrived_shared(k, 1 - half)
            arrived_shared(k, half)
        else:
            arrived(k, QM)
            arrived(k, PP)
        combined(k, QM, PP, gath.at[k, 0, col], store(gath.at[k + 1, 0, col]))
        gather_start(k + 1, 0)
        if not last:
            if not shared:
                arrived(k, PM)
            single(k, PM, 0, store(gath.at[k + 1, 1, col]))
            gather_start(k + 1, 1)
            if not shared:
                arrived(k, QP)
            single(k, QP, 1, store(gath.at[k + 1, 2, col]))
            gather_start(k + 1, 2)
        if k == 0:
            right_side(k)
    gather_finish(LEVELS, 0, dh, dl, 0)
    arrived(LEVELS - 1, YM)
    arrived(LEVELS - 1, YP)
    swap_finish(1)
    combined(LEVELS - 1, YM, YP, swap.at[1, odd], store(bcur.at[LEVELS % 2]))
    apply_narrow(bcur.at[LEVELS % 2], store(o_ref))
    for copy in started:
        copy.wait_send()
    rest = pl.ds(0, (cycle - 1) * slots)
    pltpu.make_async_copy(out_v.at[rest, :], out_v.at[rest, :], ps.at[0]).wait()

    @pl.when(odd == 1)
    def _():
        pltpu.make_async_copy(block_of(out_v, blk), block_of(in_v, blk), ps.at[4]).wait()

    rest = pl.ds(0, cycle - 1)
    pltpu.make_async_copy(out_m.at[rest], out_m.at[rest], ps.at[2]).wait()


def on_device(lower_part, diag_part, upper_part, right_side, extra, owners, rows_in, counts):
    n, c = diag_part.shape[1:]
    entries = extra.shape[0]
    cycle = lax.axis_size("blk")
    slots = 2 * entries // cycle
    vmem = pl.BlockSpec(memory_space=pltpu.VMEM)
    out = pl.pallas_call(
        kernel,
        name="levels",
        out_shape=jax.ShapeDtypeStruct((n, c), F32),
        in_specs=[vmem] * 8,
        out_specs=vmem,
        scratch_shapes=[
            pltpu.VMEM((LEVELS + 1, 3, 4, n, c), F32),
            pltpu.VMEM((LEVELS, 3, n, c), F32),
            pltpu.VMEM((LEVELS, 6, n, c), F32),
            pltpu.VMEM((n, n), BF16),
            pltpu.VMEM((n, n), BF16),
            pltpu.VMEM((2, n, 2 * n), BF16),
            pltpu.VMEM((2, n, 2 * n), BF16),
            pltpu.VMEM((n, 2 * c), BF16),
            pltpu.VMEM((n, 2 * c), BF16),
            pltpu.VMEM((n, 2 * c), BF16),
            pltpu.VMEM((n, 2 * c), BF16),
            pltpu.VMEM((n, 2 * c), F32),
            pltpu.VMEM((2 * n, 2 * c), BF16),
            pltpu.VMEM((2, n, c), F32),
            pltpu.VMEM((cycle * slots, c), F32),
            pltpu.VMEM((cycle, 1, 128), F32),
            pltpu.VMEM((cycle * slots, c), F32),
            pltpu.VMEM((cycle, 1, 128), F32),
            pltpu.VMEM((2, 2, n, c), F32),
            pltpu.SemaphoreType.DMA((LEVELS + 1, 3, 3)),
            pltpu.SemaphoreType.DMA((LEVELS + 1, 3, 3)),
            pltpu.SemaphoreType.DMA((LEVELS, 3, 2)),
            pltpu.SemaphoreType.DMA((LEVELS, 6)),
            pltpu.SemaphoreType.DMA((5,)),
            pltpu.SemaphoreType.DMA((2,)),
            pltpu.SemaphoreType.DMA((2,)),
        ],
        compiler_params=pltpu.CompilerParams(
            collective_id=0, has_side_effects=True, vmem_limit_bytes=56 * 2**20
        ),
    )(lower_part[0], diag_part[0], upper_part[0], right_side[0], extra,
      owners.reshape(1, entries), rows_in.reshape(1, entries), counts.reshape(1, 1))
    return out[None]


def solution(mesh):
    placed = (
        P("blk", None, "az"),
        P("blk", None, "az"),
        P("blk", None, "az"),
        P("blk", None, "az"),
        P("blk", "az"),
        P("blk", None),
        P("blk"),
        P("blk"),
    )
    return jax.shard_map(
        on_device, mesh=mesh, in_specs=placed, out_specs=P("blk", None, "az"), check_vma=False
    )
```

time: 259 us -> 203 us (0.78)
  the two profiles are of different devices: /device:TPU:173 before, /device:TPU:29 now
where the time goes in v1:
time: 203 us; the launch traced here: 202 us
  Pallas kernels  200 us (99%)
    pallas_call x1, Pallas kernels, on_device(): pl.pallas_call(kernel, name='levels', out_shape=jax.ShapeDtypeStruct((n,...  200 us

profile of v1, /device:TPU:29, one launch (start us, length us, event | category | flops | bytes accessed | tf_op | source)
XLA Modules:
  0.0 202.5 jit_solution(13457281632438765320)
XLA Ops:
  0.7 200.1 %levels.1 = f32[512,128]{1,0:T(8,128)} custom-call(f32[512,128]{1,0:T(8,128)} %bitcast.10, f32[512,128]{1,0:T(8,128)} %bitcast.11, f32[512,128]{1,0:T(8,128)} %bitcast.12, f32[512,128]{1,0:T(8,128)} %bitcast.13, f32[512,128]{1,0:T(8,128)} %x_ref.1, s32[1,512]{1,0:T(1,128)} %bitcast.14, s32[1,512]{1,0:T(1,128)} %bitcast.15, s32[1,1]{1,0:T(1,128)} %bitcast.8.cnt_ref), custom_call_target="tpu_custom_call" | custom-call | tf_op jit(solution)/shard_map/levels/pallas_call | solution.py:432
  200.8 1.7 copy.11

commit v2 on v1

--- a/solution.py
+++ b/solution.py
@@ -78,7 +78,7 @@
         one.start()
         started.extend([one, two])
 
-    def gather_finish(k, m, into_h, into_l, base):
+    def gather_finish(k, m, into_h, into_l, base, between=None):
         mine = az if k == 0 else col
         beside = (mine // 2) * 2 + 1 - mine % 2
 
@@ -91,6 +91,8 @@
         put(mine)
         gather_copy(k, m, 0, beside, (blk, mate)).wait_recv()
         put(beside)
+        if between is not None:
+            between()
         gather_copy(k, m, 1, (mine + 2) % 4, (blk, across)).wait_recv()
         three = gather_copy(k, m, 2, (mine + 2) % 4, (blk, mate))
         three.start()
@@ -158,6 +160,26 @@
         copy.start()
         started.append(copy)
 
+    def send_last(k):
+        copy = pltpu.make_async_remote_copy(
+            src_ref=sent.at[k, 2], dst_ref=got.at[k, 2 + 3 * odd],
+            send_sem=es.at[k, 2, 0], recv_sem=er.at[k, 2 + 3 * odd],
+            device_id=((blk + RING * (1 - 2 * odd) + cycle) % cycle, col), device_id_type=MESH,
+        )
+        copy.start()
+        started.append(copy)
+
+    def pass_last(k):
+        direct = 2 + 3 * (1 - odd)
+        arrived(k, direct)
+        copy = pltpu.make_async_remote_copy(
+            src_ref=got.at[k, direct], dst_ref=got.at[k, 2 + 3 * odd],
+            send_sem=es.at[k, 2, 1], recv_sem=er.at[k, 2 + 3 * odd],
+            device_id=((blk + 2 * RING * (1 - 2 * odd) + cycle) % cycle, az), device_id_type=MESH,
+        )
+        copy.start()
+        started.append(copy)
+
     def arrived_shared(k, slot):
         arrived(k, half * 3 + slot)
 
@@ -168,7 +190,7 @@
             vl[:, part * c : (part + 1) * c] = lo
 
         def times(rows, hi, lo):
-            return mm(dh[rows, :], hi) + mm(dh[rows, :], lo) + mm(dl[rows, :], hi)
+            return mm(dh[k % 2, rows, :], hi) + mm(dh[k % 2, rows, :], lo) + mm(dl[k % 2, rows, :], hi)
 
         def base(rows):
             return jnp.concatenate([gath[k, 1, col, rows, :], gath[k, 2, col, rows, :]], axis=1)
@@ -192,16 +214,16 @@
     def put_pair(ref, rows, x):
         ref[rows, :c], ref[rows, c:] = halves(x)
 
-    def apply_narrow(v_ref, write):
+    def apply_narrow(k, v_ref, write):
         put_pair(vh, slice(None), v_ref[...])
         for rows in tiles:
-            put_pair(xh, rows, 2.0 * v_ref[rows, :] - narrow(rows, dh, dl, vh[...]))
-        for rows in tiles:
-            w = 2.0 * v_ref[rows, :] - narrow(rows, dh, dl, xh[...])
+            put_pair(xh, rows, 2.0 * v_ref[rows, :] - narrow(rows, dh.at[k % 2], dl.at[k % 2], vh[...]))
+        for rows in tiles:
+            w = 2.0 * v_ref[rows, :] - narrow(rows, dh.at[k % 2], dl.at[k % 2], xh[...])
             w_ref[rows, :c] = w
             put_pair(vh, rows, w)
         for rows in tiles:
-            write(rows, 2.0 * w_ref[rows, :c] - narrow(rows, dh, dl, vh[...]))
+            write(rows, 2.0 * w_ref[rows, :c] - narrow(rows, dh.at[k % 2], dl.at[k % 2], vh[...]))
 
     def combined(k, first, second, old, write):
         p = k % 2
@@ -317,7 +339,13 @@
         gather_start(0, m)
 
     PM, QM, YM, PP, QP, YP = range(6)
-    rhs = []
+    def drain(copies):
+        for copy in copies:
+            copy.wait_send()
+        started[:] = [copy for copy in started if not any(copy is other for other in copies)]
+
+
+    ahead = []
 
     def right_side(k):
         s = 2**k
@@ -335,56 +363,55 @@
             combined(k - 1, YM, YP, bcur.at[(k - 1) % 2], store(bcur.at[k % 2]))
         if last:
             swap_start(1, bcur.at[k % 2])
-        apply_narrow(bcur.at[k % 2], store(sent.at[k, 2]))
-        if shared:
+        apply_narrow(k, bcur.at[k % 2], store(sent.at[k, 2]))
+        if last:
+            drain(ahead)
+        if last:
+            send_last(k)
+        elif shared:
             send_shared(k, 2)
         else:
-            rhs[:] = [
-                send(k, YM, 2, (upper(s), col) if last else at(upper(s))),
-                send(k, YP, 2, (lower(s), col) if last else at(lower(s))),
-            ]
+            send(k, YM, 2, at(upper(s)))
+            send(k, YP, 2, at(lower(s)))
 
     for k in range(LEVELS):
         s = 2**k
         last = k == LEVELS - 1
         shared = s == RING // 2
-        gather_finish(k, 0, dh, dl, 0)
-        if s == RING:
-            pass_on(k - 1, 2)
+        gather_finish(k, 0, dh.at[k % 2], dl.at[k % 2], 0, (lambda: pass_on(2, 2)) if s == RING else None)
         if k == 0:
             gather_finish(k, 1, luh.at[k % 2], lul.at[k % 2], 0)
-            apply_narrow(gath.at[k, 1, col], store(sent.at[k, 0]))
+            apply_narrow(k, gath.at[k, 1, col], store(sent.at[k, 0]))
             send(k, PP, 0, at(lower(s)))
             send(k, PM, 0, at(upper(s)))
+            gather_finish(k, 2, luh.at[k % 2], lul.at[k % 2], n)
+            apply_narrow(k, gath.at[k, 2, col], store(sent.at[k, 1]))
+            send(k, QM, 1, at(upper(s)))
+            send(k, QP, 1, at(lower(s)))
             swap_start(0, b_ref)
             deliver()
-            gather_finish(k, 2, luh.at[k % 2], lul.at[k % 2], n)
-            apply_narrow(gath.at[k, 2, col], store(sent.at[k, 1]))
-            send(k, QM, 1, at(upper(s)))
-            send(k, QP, 1, at(lower(s)))
         else:
             apply_wide(k)
         if k == 0:
             pass
         elif shared:
-            for copy in rhs:
-                copy.wait_send()
-            started[:] = [copy for copy in started if not any(copy is other for other in rhs)]
             send_shared(k, half)
             send_shared(k, 1 - half)
         else:
-            send(k, QM, 1, at(upper(s)))
-            send(k, PP, 0, at(lower(s)))
+            ahead[:] = [send(k, QM, 1, at(upper(s))), send(k, PP, 0, at(lower(s)))]
             if not last:
                 send(k, PM, 0, at(upper(s)))
                 send(k, QP, 1, at(lower(s)))
-        if k > 0:
-            right_side(k)
+        if k == 1:
+            right_side(0)
         if k > 0:
             gather_finish(k, 1, luh.at[k % 2], lul.at[k % 2], 0)
             gather_finish(k, 2, luh.at[k % 2], lul.at[k % 2], n)
+        if last:
+            right_side(k)
         if shared:
             pass_on(k, 1 - half)
+            right_side(k)
             pass_on(k, half)
             arrived_shared(k, 1 - half)
             arrived_shared(k, half)
@@ -402,14 +429,13 @@
                 arrived(k, QP)
             single(k, QP, 1, store(gath.at[k + 1, 2, col]))
             gather_start(k + 1, 2)
-        if k == 0:
-            right_side(k)
-    gather_finish(LEVELS, 0, dh, dl, 0)
-    arrived(LEVELS - 1, YM)
-    arrived(LEVELS - 1, YP)
+            if k > 0 and not shared:
+                right_side(k)
+    gather_finish(LEVELS, 0, dh.at[LEVELS % 2], dl.at[LEVELS % 2], 0, lambda: pass_last(LEVELS - 1))
+    arrived(LEVELS - 1, 2 + 3 * odd)
     swap_finish(1)
     combined(LEVELS - 1, YM, YP, swap.at[1, odd], store(bcur.at[LEVELS % 2]))
-    apply_narrow(bcur.at[LEVELS % 2], store(o_ref))
+    apply_narrow(LEVELS, bcur.at[LEVELS % 2], store(o_ref))
     for copy in started:
         copy.wait_send()
     rest = pl.ds(0, (cycle - 1) * slots)
@@ -439,8 +465,8 @@
             pltpu.VMEM((LEVELS + 1, 3, 4, n, c), F32),
             pltpu.VMEM((LEVELS, 3, n, c), F32),
             pltpu.VMEM((LEVELS, 6, n, c), F32),
-            pltpu.VMEM((n, n), BF16),
-            pltpu.VMEM((n, n), BF16),
+            pltpu.VMEM((2, n, n), BF16),
+            pltpu.VMEM((2, n, n), BF16),
             pltpu.VMEM((2, n, 2 * n), BF16),
             pltpu.VMEM((2, n, 2 * n), BF16),
             pltpu.VMEM((n, 2 * c), BF16),

time: 203 us -> 197 us (0.970)
  the two profiles are of different devices: /device:TPU:29 before, /device:TPU:34 now
where the time goes in v2:
time: 197 us; the launch traced here: 196 us
  Pallas kernels  193 us (98%)
    pallas_call x1, Pallas kernels, on_device(): pl.pallas_call(kernel, name='levels', out_shape=jax.ShapeDtypeStruct((n,...  193 us

profile of v2, /device:TPU:34, one launch (start us, length us, event | category | flops | bytes accessed | tf_op | source)
XLA Modules:
  0.0 195.6 jit_solution(13500915184665402973)
XLA Ops:
  0.7 193.3 %levels.1 = f32[512,128]{1,0:T(8,128)} custom-call(f32[512,128]{1,0:T(8,128)} %bitcast.10, f32[512,128]{1,0:T(8,128)} %bitcast.11, f32[512,128]{1,0:T(8,128)} %bitcast.12, f32[512,128]{1,0:T(8,128)} %bitcast.13, f32[512,128]{1,0:T(8,128)} %x_ref.1, s32[1,512]{1,0:T(1,128)} %bitcast.14, s32[1,512]{1,0:T(1,128)} %bitcast.15, s32[1,1]{1,0:T(1,128)} %bitcast.8.cnt_ref), custom_call_target="tpu_custom_call" | custom-call | tf_op jit(solution)/shard_map/levels/pallas_call | solution.py:458
  194.0 1.7 copy.11

commit v3 on v2

--- a/solution.py
+++ b/solution.py
@@ -337,6 +337,7 @@
     pl.semaphore_wait(barrier, 2 * cycle)
     for m in range(3):
         gather_start(0, m)
+    swap_start(0, b_ref)
 
     PM, QM, YM, PP, QP, YP = range(6)
     def drain(copies):
@@ -378,7 +379,7 @@
         s = 2**k
         last = k == LEVELS - 1
         shared = s == RING // 2
-        gather_finish(k, 0, dh.at[k % 2], dl.at[k % 2], 0, (lambda: pass_on(2, 2)) if s == RING else None)
+        gather_finish(k, 0, dh.at[k % 2], dl.at[k % 2], 0)
         if k == 0:
             gather_finish(k, 1, luh.at[k % 2], lul.at[k % 2], 0)
             apply_narrow(k, gath.at[k, 1, col], store(sent.at[k, 0]))
@@ -388,7 +389,6 @@
             apply_narrow(k, gath.at[k, 2, col], store(sent.at[k, 1]))
             send(k, QM, 1, at(upper(s)))
             send(k, QP, 1, at(lower(s)))
-            swap_start(0, b_ref)
             deliver()
         else:
             apply_wide(k)
@@ -402,16 +402,14 @@
             if not last:
                 send(k, PM, 0, at(upper(s)))
                 send(k, QP, 1, at(lower(s)))
-        if k == 1:
-            right_side(0)
         if k > 0:
+            right_side(k - 1)
             gather_finish(k, 1, luh.at[k % 2], lul.at[k % 2], 0)
             gather_finish(k, 2, luh.at[k % 2], lul.at[k % 2], n)
-        if last:
-            right_side(k)
+        if s == RING:
+            pass_on(k - 1, 2)
         if shared:
             pass_on(k, 1 - half)
-            right_side(k)
             pass_on(k, half)
             arrived_shared(k, 1 - half)
             arrived_shared(k, half)
@@ -429,9 +427,9 @@
                 arrived(k, QP)
             single(k, QP, 1, store(gath.at[k + 1, 2, col]))
             gather_start(k + 1, 2)
-            if k > 0 and not shared:
-                right_side(k)
-    gather_finish(LEVELS, 0, dh.at[LEVELS % 2], dl.at[LEVELS % 2], 0, lambda: pass_last(LEVELS - 1))
+    right_side(LEVELS - 1)
+    gather_finish(LEVELS, 0, dh.at[LEVELS % 2], dl.at[LEVELS % 2], 0)
+    pass_last(LEVELS - 1)
     arrived(LEVELS - 1, 2 + 3 * odd)
     swap_finish(1)
     combined(LEVELS - 1, YM, YP, swap.at[1, odd], store(bcur.at[LEVELS % 2]))

time: 197 us -> 187 us (0.949)
  Pallas kernels: 193 us -> 182 us
    pallas_call x1, Pallas kernels: 193 us -> 182 us  [on_device(): pl.pallas_call(kernel, name='levels', out_shape=jax.ShapeDtypeStruct((n,...]
where the time goes in v3:
time: 187 us; the launch traced here: 185 us
  Pallas kernels  182 us (97%)
    pallas_call x1, Pallas kernels, on_device(): pl.pallas_call(kernel, name='levels', out_shape=jax.ShapeDtypeStruct((n,...  182 us

profile of v3, /device:TPU:34, one launch (start us, length us, event | category | flops | bytes accessed | tf_op | source)
XLA Modules:
  0.0 184.5 jit_solution(13801890525099192029)
XLA Ops:
  0.7 182.2 %levels.1 = f32[512,128]{1,0:T(8,128)} custom-call(f32[512,128]{1,0:T(8,128)} %bitcast.10, f32[512,128]{1,0:T(8,128)} %bitcast.11, f32[512,128]{1,0:T(8,128)} %bitcast.12, f32[512,128]{1,0:T(8,128)} %bitcast.13, f32[512,128]{1,0:T(8,128)} %x_ref.1, s32[1,512]{1,0:T(1,128)} %bitcast.14, s32[1,512]{1,0:T(1,128)} %bitcast.15, s32[1,1]{1,0:T(1,128)} %bitcast.8.cnt_ref), custom_call_target="tpu_custom_call" | custom-call | tf_op jit(solution)/shard_map/levels/pallas_call | solution.py:456
  182.8 1.7 copy.11

commit v4 on v3

--- a/solution.py
+++ b/solution.py
@@ -403,7 +403,8 @@
                 send(k, PM, 0, at(upper(s)))
                 send(k, QP, 1, at(lower(s)))
         if k > 0:
-            right_side(k - 1)
+            if not last:
+                right_side(k - 1)
             gather_finish(k, 1, luh.at[k % 2], lul.at[k % 2], 0)
             gather_finish(k, 2, luh.at[k % 2], lul.at[k % 2], n)
         if s == RING:
@@ -427,6 +428,8 @@
                 arrived(k, QP)
             single(k, QP, 1, store(gath.at[k + 1, 2, col]))
             gather_start(k + 1, 2)
+            if shared:
+                right_side(k)
     right_side(LEVELS - 1)
     gather_finish(LEVELS, 0, dh.at[LEVELS % 2], dl.at[LEVELS % 2], 0)
     pass_last(LEVELS - 1)

time: 187 us -> 190 us (1.016); the launches traced: 185 us -> 190 us
  Pallas kernels: 182 us -> 188 us
    pallas_call x1, Pallas kernels: 182 us -> 188 us  [on_device(): pl.pallas_call(kernel, name='levels', out_shape=jax.ShapeDtypeStruct((n,...]
where the time goes in v4:
time: 190 us
  Pallas kernels  188 us (99%)
    pallas_call x1, Pallas kernels, on_device(): pl.pallas_call(kernel, name='levels', out_shape=jax.ShapeDtypeStruct((n,...  188 us

profile of v4, /device:TPU:34, one launch (start us, length us, event | category | flops | bytes accessed | tf_op | source)
XLA Modules:
  0.0 189.9 jit_solution(14745320211462691624)
XLA Ops:
  0.7 187.6 %levels.1 = f32[512,128]{1,0:T(8,128)} custom-call(f32[512,128]{1,0:T(8,128)} %bitcast.10, f32[512,128]{1,0:T(8,128)} %bitcast.11, f32[512,128]{1,0:T(8,128)} %bitcast.12, f32[512,128]{1,0:T(8,128)} %bitcast.13, f32[512,128]{1,0:T(8,128)} %x_ref.1, s32[1,512]{1,0:T(1,128)} %bitcast.14, s32[1,512]{1,0:T(1,128)} %bitcast.15, s32[1,1]{1,0:T(1,128)} %bitcast.8.cnt_ref), custom_call_target="tpu_custom_call" | custom-call | tf_op jit(solution)/shard_map/levels/pallas_call | solution.py:459
  188.2 1.7 copy.11
